TPU v7x, 32 devices: a whole 2x2x4 slice. The times are simulated.
32 devices in a mesh: patch: 8 (over z, x), lev: 4 (over y, core).
Axes of the slice: x: 2, y: 2, z: 4, core: 2. Of those that a mesh axis runs over, the one named last changes fastest.
Arguments:
- tracer_field: float32 [80, 3, 16384], P('lev', None, 'patch'), may hold values from -6 to 6
- send_coarse1: int32 [8, 2, 128], P('patch'), may hold values from 0 to 1023
- send_detail1: int32 [8, 2, 128], P('patch'), may hold values from 0 to 1023
- send_coarse2: int32 [8, 2, 64], P('patch'), may hold values from 0 to 511
- send_detail2: int32 [8, 2, 64], P('patch'), may hold values from 0 to 511
- predict_links1: int32 [8, 8192], P(None, 'patch'), may hold values from 0 to 1279
- predict_weights1: float32 [8, 8192], P(None, 'patch'), may hold values from 0.02 to 0.22
- update_links1: int32 [8, 8192], P(None, 'patch'), may hold values from 0 to 1279
- update_weights1: float32 [8, 8192], P(None, 'patch'), may hold values from 0.02 to 0.14
- predict_links2: int32 [8, 4096], P(None, 'patch'), may hold values from 0 to 639
- predict_weights2: float32 [8, 4096], P(None, 'patch'), may hold values from 0.02 to 0.22
- update_links2: int32 [8, 4096], P(None, 'patch'), may hold values from 0 to 639
- update_weights2: float32 [8, 4096], P(None, 'patch'), may hold values from 0.02 to 0.14
Outputs:
- coefficients: float32 [80, 3, 16384], P(None, None, ('patch', 'lev'))
Inputs may be any that keep to these rules, and one draw needn't show every extreme that they name: `send_coarse1`: row lists index a patch's own coarse or detail rows of that level. `predict_links1`: links index the patch's own rows first, then the 128 rows from the left neighbour, then the 128 from the right. `predict_links2`: links index the patch's own rows first, then the 64 rows from the left neighbour, then the 64 from the right.
All inputs are finite; a program needn't handle non-finite values.
Results may differ from a plain program's by a relative error of at most 0.00007.
Values sent between devices are 32-bit elements; how exact they have to be, the bound alone decides.
A program may use at most 64 MiB of HBM per device.

v0:
```python
import jax
import jax.numpy as jnp
from jax import lax
from jax.sharding import PartitionSpec as P

LEVELS = 80


def passed_along(block, axis, distance):
    devices = range(lax.axis_size(axis))
    route = [((i - distance) % len(devices), i) for i in devices]
    return lax.ppermute(block, axis, route)


def cosine_table(length):
    rows = jnp.arange(length).astype(jnp.float32)[:, None]
    columns = jnp.arange(length).astype(jnp.float32)[None, :]
    matrix = jnp.cos(jnp.pi * (columns + 0.5) * rows / length) * jnp.sqrt(2.0 / length)
    first = jnp.where(rows == 0.0, jnp.sqrt(0.5), 1.0)
    return matrix * first


def extend(values, send_rows):
    first = values[:, :, send_rows[0]]
    second = values[:, :, send_rows[1]]
    from_left = passed_along(second, "patch", 1)
    from_right = passed_along(first, "patch", -1)
    return jnp.concatenate([values, from_left, from_right], axis=2)


def weighted(extended, links, weights):
    total = jnp.zeros(extended.shape[:2] + (links.shape[1],), jnp.float32)
    for neighbour in range(links.shape[0]):
        picked = jnp.take(extended, links[neighbour], axis=2)
        total = total + weights[neighbour][None, None, :] * picked
    return total


def lift(
    values, send_coarse, send_detail, predict_links, predict_weights, update_links, update_weights
):
    half_cells = values.shape[2] // 2
    fine_part = values[:, :, :half_cells]
    coarse = values[:, :, half_cells:]
    detail = fine_part - weighted(extend(coarse, send_coarse[0]), predict_links, predict_weights)
    smooth = coarse + weighted(extend(detail, send_detail[0]), update_links, update_weights)
    return (detail, smooth)


def on_device(
    tracer_field,
    send_coarse1,
    send_detail1,
    send_coarse2,
    send_detail2,
    predict_links1,
    predict_weights1,
    update_links1,
    update_weights1,
    predict_links2,
    predict_weights2,
    update_links2,
    update_weights2,
):
    detail1, smooth1 = lift(
        tracer_field,
        send_coarse1,
        send_detail1,
        predict_links1,
        predict_weights1,
        update_links1,
        update_weights1,
    )
    detail2, smooth2 = lift(
        smooth1,
        send_coarse2,
        send_detail2,
        predict_links2,
        predict_weights2,
        update_links2,
        update_weights2,
    )
    bands = jnp.concatenate([detail1, detail2, smooth2], axis=2)
    table = cosine_table(LEVELS)
    return jnp.einsum(
        "km,mtc->ktc",
        table,
        lax.all_to_all(bands, "lev", split_axis=2, concat_axis=0, tiled=True),
        precision=lax.Precision.HIGHEST,
    )


def solution(mesh):
    in_specs = (
        P("lev", None, "patch"),
        P("patch", None, None),
        P("patch", None, None),
        P("patch", None, None),
        P("patch", None, None),
        P(None, "patch"),
        P(None, "patch"),
        P(None, "patch"),
        P(None, "patch"),
        P(None, "patch"),
        P(None, "patch"),
        P(None, "patch"),
        P(None, "patch"),
    )
    out_specs = P(None, None, ("patch", "lev"))
    return jax.shard_map(
        on_device, mesh=mesh, in_specs=in_specs, out_specs=out_specs, check_vma=False
    )
```

profile of v0, /device:TPU:0, one launch (start us, length us, event | category | flops | bytes accessed | tf_op | source)
XLA Modules:
  0.0 317.7 jit_solution(586208414387736212)
XLA Ops:
  3.6 3.0 collective-permute-start
  7.5 3.1 collective-permute-start.1
  39.8 8.0 %gather_fusion.8 = f32[1024,20,3]{1,2,0:T(4,128)} fusion(f32[20,3,1280]{0,1,2:T(4,128)S(1)} %copy.142, s32[1024]{0:T(1024)S(1)} %fusion.41), kind=kCustom, calls=%fused_computation.clone | custom fusion | bytes 495616 | tf_op jit(solution)/shard_map/jit(_take)/gather | solution.py:34
  49.5 8.0 %gather_fusion.9 = f32[1024,20,3]{1,2,0:T(4,128)} fusion(f32[20,3,1280]{0,1,2:T(4,128)S(1)} %copy.142, s32[1024]{0:T(1024)S(1)} %fusion.42), kind=kCustom, calls=%fused_computation.2.clone | custom fusion | bytes 495616 | tf_op jit(solution)/shard_map/jit(_take)/gather | solution.py:34
  57.5 2.5 copy.145
  60.0 8.0 %gather_fusion.10 = f32[1024,20,3]{1,2,0:T(4,128)} fusion(f32[20,3,1280]{0,1,2:T(4,128)S(1)} %copy.142, s32[1024]{0:T(1024)S(1)} %fusion.43), kind=kCustom, calls=%fused_computation.3.clone | custom fusion | bytes 495616 | tf_op jit(solution)/shard_map/jit(_take)/gather | solution.py:34
  68.0 2.5 copy.147
  70.4 8.0 %gather_fusion.11 = f32[1024,20,3]{1,2,0:T(4,128)} fusion(f32[20,3,1280]{0,1,2:T(4,128)S(1)} %copy.142, s32[1024]{0:T(1024)S(1)} %fusion.44), kind=kCustom, calls=%fused_computation.4.clone | custom fusion | bytes 495616 | tf_op jit(solution)/shard_map/jit(_take)/gather | solution.py:34
  78.4 2.5 copy.149
  80.9 8.0 %gather_fusion.12 = f32[1024,20,3]{1,2,0:T(4,128)} fusion(f32[20,3,1280]{0,1,2:T(4,128)S(1)} %copy.142, s32[1024]{0:T(1024)S(1)} %fusion.45), kind=kCustom, calls=%fused_computation.5.clone | custom fusion | bytes 495616 | tf_op jit(solution)/shard_map/jit(_take)/gather | solution.py:34
  88.9 2.5 copy.151
  91.3 8.0 %gather_fusion.13 = f32[1024,20,3]{1,2,0:T(4,128)} fusion(f32[20,3,1280]{0,1,2:T(4,128)S(1)} %copy.142, s32[1024]{0:T(1024)S(1)} %fusion.46), kind=kCustom, calls=%fused_computation.6.clone | custom fusion | bytes 495616 | tf_op jit(solution)/shard_map/jit(_take)/gather | solution.py:34
  99.3 2.5 copy.153
  101.8 8.0 %gather_fusion.14 = f32[1024,20,3]{1,2,0:T(4,128)} fusion(f32[20,3,1280]{0,1,2:T(4,128)S(1)} %copy.142, s32[1024]{0:T(1024)S(1)} %fusion.47), kind=kCustom, calls=%fused_computation.7.clone | custom fusion | bytes 495616 | tf_op jit(solution)/shard_map/jit(_take)/gather | solution.py:34
  109.8 2.5 copy.155
  112.2 8.2 %gather_fusion.15 = f32[1024,20,3]{1,2,0:T(4,128)} fusion(f32[20,3,1280]{0,1,2:T(4,128)S(1)} %copy.142, s32[1024]{0:T(1024)} %fusion.48), kind=kCustom, calls=%fused_computation.8.clone | custom fusion | bytes 495616 | tf_op jit(solution)/shard_map/jit(_take)/gather | solution.py:34
  126.0 4.8 %collective-permute-start.3 = (f32[20,3,128]{2,0,1:T(8,128)S(1)}, f32[20,3,128]{2,0,1:T(8,128)S(1)}, u32[]{:S(2)}, u32[]{:S(2)}) collective-permute-start(f32[20,3,128]{2,0,1:T(8,128)S(1)} %bitcast.304), channel_id=1, source_target_pairs={{4,0},{8,4},{12,8},{16,12},{20,16},{24,20},{28,24},{0,28},{5,1},{9... | collective-permute-start | bytes 92168 | tf_op jit(solution)/shard_map/ppermute | solution.py:12
  133.5 8.0 %gather_fusion.16 = f32[1024,20,3]{1,2,0:T(4,128)} fusion(f32[20,3,1280]{0,1,2:T(4,128)S(1)} %copy.162, s32[1024]{0:T(1024)S(1)} %copy-done.29), kind=kCustom, calls=%fused_computation.9.clone | custom fusion | bytes 495616 | tf_op jit(solution)/shard_map/jit(_take)/gather | solution.py:34
  141.5 2.5 copy.163
  143.9 8.0 %gather_fusion.17 = f32[1024,20,3]{1,2,0:T(4,128)} fusion(f32[20,3,1280]{0,1,2:T(4,128)S(1)} %copy.162, s32[1024]{0:T(1024)S(1)} %copy-done.28), kind=kCustom, calls=%fused_computation.10.clone | custom fusion | bytes 495616 | tf_op jit(solution)/shard_map/jit(_take)/gather | solution.py:34
  151.9 2.5 copy.165
  154.4 8.0 %gather_fusion.18 = f32[1024,20,3]{1,2,0:T(4,128)} fusion(f32[20,3,1280]{0,1,2:T(4,128)S(1)} %copy.162, s32[1024]{0:T(1024)S(1)} %copy-done.27), kind=kCustom, calls=%fused_computation.11.clone | custom fusion | bytes 495616 | tf_op jit(solution)/shard_map/jit(_take)/gather | solution.py:34
  162.4 2.5 copy.167
  164.8 8.0 %gather_fusion.19 = f32[1024,20,3]{1,2,0:T(4,128)} fusion(f32[20,3,1280]{0,1,2:T(4,128)S(1)} %copy.162, s32[1024]{0:T(1024)S(1)} %copy-done.26), kind=kCustom, calls=%fused_computation.12.clone | custom fusion | bytes 495616 | tf_op jit(solution)/shard_map/jit(_take)/gather | solution.py:34
  172.8 2.5 copy.169
  175.3 8.0 %gather_fusion.20 = f32[1024,20,3]{1,2,0:T(4,128)} fusion(f32[20,3,1280]{0,1,2:T(4,128)S(1)} %copy.162, s32[1024]{0:T(1024)S(1)} %copy-done.25), kind=kCustom, calls=%fused_computation.13.clone | custom fusion | bytes 495616 | tf_op jit(solution)/shard_map/jit(_take)/gather | solution.py:34
  183.2 2.5 copy.171
  185.7 8.0 %gather_fusion.21 = f32[1024,20,3]{1,2,0:T(4,128)} fusion(f32[20,3,1280]{0,1,2:T(4,128)S(1)} %copy.162, s32[1024]{0:T(1024)S(1)} %copy-done.24), kind=kCustom, calls=%fused_computation.14.clone | custom fusion | bytes 495616 | tf_op jit(solution)/shard_map/jit(_take)/gather | solution.py:34
  193.7 2.5 copy.173
  196.2 8.0 %gather_fusion.22 = f32[1024,20,3]{1,2,0:T(4,128)} fusion(f32[20,3,1280]{0,1,2:T(4,128)S(1)} %copy.162, s32[1024]{0:T(1024)S(1)} %copy-done.23), kind=kCustom, calls=%fused_computation.15.clone | custom fusion | bytes 495616 | tf_op jit(solution)/shard_map/jit(_take)/gather | solution.py:34
  204.2 2.5 copy.175
  206.7 8.0 %gather_fusion.23 = f32[1024,20,3]{1,2,0:T(4,128)} fusion(f32[20,3,1280]{0,1,2:T(4,128)S(1)} %copy.162, s32[1024]{0:T(1024)S(1)} %copy-done.22), kind=kCustom, calls=%fused_computation.16.clone | custom fusion | bytes 495616 | tf_op jit(solution)/shard_map/jit(_take)/gather | solution.py:34
  214.7 2.6 copy.177
  221.3 5.1 %collective-permute-start.5 = (f32[20,3,64]{2,0,1:T(8,128)S(1)}, f32[20,3,64]{2,0,1:T(8,128)S(1)}, u32[]{:S(2)}, u32[]{:S(2)}) collective-permute-start(f32[20,3,64]{2,0,1:T(8,128)S(1)} %bitcast.339), channel_id=1, source_target_pairs={{4,0},{8,4},{12,8},{16,12},{20,16},{24,20},{28,24},{0,28},{5,1},{9... | collective-permute-start | bytes 46088 | tf_op jit(solution)/shard_map/ppermute | solution.py:12
  228.6 2.1 gather_fusion.24
  231.0 2.1 gather_fusion.25
  233.4 2.1 gather_fusion.26
  235.8 2.1 gather_fusion.27
  254.0 5.3 %collective-permute-start.7 = (f32[20,3,64]{2,0,1:T(8,128)S(1)}, f32[20,3,64]{2,0,1:T(8,128)S(1)}, u32[]{:S(2)}, u32[]{:S(2)}) collective-permute-start(f32[20,3,64]{2,0,1:T(8,128)S(1)} %bitcast.340), channel_id=1, source_target_pairs={{4,0},{8,4},{12,8},{16,12},{20,16},{24,20},{28,24},{0,28},{5,1},{9... | collective-permute-start | bytes 46088 | tf_op jit(solution)/shard_map/ppermute | solution.py:12
  263.9 2.1 gather_fusion.33
  266.3 2.1 gather_fusion.34
  268.7 2.1 gather_fusion.35
  284.7 3.1 copy.218
  287.8 5.4 %reshape.717 = f32[4,1,30720]{2,1,0:T(1,128)} reshape(f32[2048,3,20]{2,1,0:T(4,128)} %bitcast.298) | data formatting | bytes 983040
  293.2 3.7 %all-to-all-start = ((f32[4,1,30720]{2,1,0:T(1,128)}), f32[4,1,30720]{2,1,0:T(1,128)S(1)}, u32[]{:S(2)}, u32[]{:S(2)}) async-start(f32[4,1,30720]{2,1,0:T(1,128)} %reshape.717), calls=%async_computation | async-start | bytes 983040 | tf_op jit(solution)/shard_map/all_to_all | solution.py:88
  297.0 8.1 %all-to-all-done = f32[4,1,30720]{2,1,0:T(1,128)S(1)} async-done(((f32[4,1,30720]{2,1,0:T(1,128)}), f32[4,1,30720]{2,1,0:T(1,128)S(1)}, u32[]{:S(2)}, u32[]{:S(2)}) %all-to-all-start) | async-done | bytes 491552 | tf_op jit(solution)/shard_map/all_to_all | solution.py:88
  307.7 5.0 %reshape.718 = f32[2048,3,20]{2,1,0:T(4,128)} reshape(f32[4,30720]{1,0:T(4,128)S(1)} %reduce) | data formatting | bytes 983040
  312.7 3.4 %copy.219 = f32[20,3,4,512]{3,0,2,1:T(8,128)S(1)} copy(f32[20,3,4,512]{0,1,3,2:T(4,128)} %bitcast.299) | data formatting | bytes 983040 | tf_op jit(solution)/shard_map/all_to_all | solution.py:88
  (307 shorter events, 89.3 us)
Async XLA Ops:
  0.0 10.6 %copy-start.14 = (s32[8,1024]{1,0:T(8,128)S(1)}, s32[8,1024]{1,0:T(8,128)}, u32[]{:S(2)}) copy-start(s32[8,1024]{1,0:T(8,128)} %param.22) | copy-start | bytes 98308
  0.0 13.6 %copy-start.15 = (s32[8,1024]{1,0:T(8,128)S(1)}, s32[8,1024]{1,0:T(8,128)}, u32[]{:S(2)}) copy-start(s32[8,1024]{1,0:T(8,128)} %param.24) | copy-start | bytes 98308
  0.0 20.8 %copy-start.30 = (s32[8,512]{1,0:T(8,128)S(1)}, s32[8,512]{1,0:T(8,128)}, u32[]{:S(2)}) copy-start(s32[8,512]{1,0:T(8,128)} %param.26) | copy-start | bytes 49156
  0.8 22.3 %copy-start.31 = (s32[8,512]{1,0:T(8,128)S(1)}, s32[8,512]{1,0:T(8,128)}, u32[]{:S(2)}) copy-start(s32[8,512]{1,0:T(8,128)} %param.28) | copy-start | bytes 49156
  0.8 26.4 %copy-start.16 = (f32[8,1024]{1,0:T(8,128)S(1)}, f32[8,1024]{1,0:T(8,128)}, u32[]{:S(2)}) copy-start(f32[8,1024]{1,0:T(8,128)} %param.23) | copy-start | bytes 98308
  0.8 27.0 %copy-start.71 = (s32[1,2,128]{2,1,0:T(2,128)S(1)}, s32[1,2,128]{2,1,0:T(2,128)}, u32[]{:S(2)}) copy-start(s32[1,2,128]{2,1,0:T(2,128)} %param.19) | copy-start | bytes 3076
  0.8 27.0 %copy-start.17 = (f32[8,1024]{1,0:T(8,128)S(1)}, f32[8,1024]{1,0:T(8,128)}, u32[]{:S(2)}) copy-start(f32[8,1024]{1,0:T(8,128)} %param.25) | copy-start | bytes 98308
  1.8 26.0 %copy-start.72 = (s32[1,2,64]{2,1,0:T(2,128)S(1)}, s32[1,2,64]{2,1,0:T(2,128)}, u32[]{:S(2)}) copy-start(s32[1,2,64]{2,1,0:T(2,128)} %param.20) | copy-start | bytes 1540
  1.8 30.8 %copy-start.32 = (f32[8,512]{1,0:T(8,128)S(1)}, f32[8,512]{1,0:T(8,128)}, u32[]{:S(2)}) copy-start(f32[8,512]{1,0:T(8,128)} %param.27) | copy-start | bytes 49156
  1.8 31.4 %copy-start.73 = (s32[1,2,64]{2,1,0:T(2,128)S(1)}, s32[1,2,64]{2,1,0:T(2,128)}, u32[]{:S(2)}) copy-start(s32[1,2,64]{2,1,0:T(2,128)} %param.21) | copy-start | bytes 1540
  1.8 33.8 %copy-start.33 = (f32[8,512]{1,0:T(8,128)S(1)}, f32[8,512]{1,0:T(8,128)}, u32[]{:S(2)}) copy-start(f32[8,512]{1,0:T(8,128)} %param.29) | copy-start | bytes 49156
  3.6 35.0 %collective-permute-start = (f32[20,3,128]{2,0,1:T(8,128)S(1)}, f32[20,3,128]{2,0,1:T(8,128)S(1)}, u32[]{:S(2)}, u32[]{:S(2)}) collective-permute-start(f32[20,3,128]{2,0,1:T(8,128)S(1)} %bitcast.301), channel_id=1, source_target_pairs={{28,0},{0,4},{4,8},{8,12},{12,16},{16,20},{20,24},{24,28},{29,1},{... | collective-permute-start | bytes 92168 | tf_op jit(solution)/shard_map/ppermute | solution.py:12
  7.5 31.2 %collective-permute-start.1 = (f32[20,3,128]{2,0,1:T(8,128)S(1)}, f32[20,3,128]{2,0,1:T(8,128)S(1)}, u32[]{:S(2)}, u32[]{:S(2)}) collective-permute-start(f32[20,3,128]{2,0,1:T(8,128)S(1)} %bitcast.302), channel_id=1, source_target_pairs={{4,0},{8,4},{12,8},{16,12},{20,16},{24,20},{28,24},{0,28},{5,1},{9... | collective-permute-start | bytes 92168 | tf_op jit(solution)/shard_map/ppermute | solution.py:12
  112.2 10.3 %copy-start = (f32[20,3,2048]{2,0,1:T(8,128)S(1)}, f32[20,3,2048]{2,0,1:T(8,128)}, u32[]{:S(2)}) copy-start(f32[20,3,2048]{2,0,1:T(8,128)} %param.17) | copy-start | bytes 1474564
  123.0 7.7 %copy-start.54 = (s32[512]{0:T(512)S(1)}, s32[512]{0:T(512)}, u32[]{:S(2)}) copy-start(s32[512]{0:T(512)} %compare_select_fusion.18) | copy-start | bytes 6148
  124.9 8.5 %copy-start.29 = (s32[1024]{0:T(1024)S(1)}, s32[1024]{0:T(1024)}, u32[]{:S(2)}) copy-start(s32[1024]{0:T(1024)} %fusion.49) | copy-start | bytes 12292
  124.9 6.7 %collective-permute-start.2 = (f32[20,3,128]{2,0,1:T(8,128)S(1)}, f32[20,3,128]{2,0,1:T(8,128)S(1)}, u32[]{:S(2)}, u32[]{:S(2)}) collective-permute-start(f32[20,3,128]{2,0,1:T(8,128)S(1)} %bitcast.303), channel_id=1, source_target_pairs={{28,0},{0,4},{4,8},{8,12},{12,16},{16,20},{20,24},{24,28},{29,1},{... | collective-permute-start | bytes 92168 | tf_op jit(solution)/shard_map/ppermute | solution.py:12
  126.0 6.4 %collective-permute-start.3 = (f32[20,3,128]{2,0,1:T(8,128)S(1)}, f32[20,3,128]{2,0,1:T(8,128)S(1)}, u32[]{:S(2)}, u32[]{:S(2)}) collective-permute-start(f32[20,3,128]{2,0,1:T(8,128)S(1)} %bitcast.304), channel_id=1, source_target_pairs={{4,0},{8,4},{12,8},{16,12},{20,16},{24,20},{28,24},{0,28},{5,1},{9... | collective-permute-start | bytes 92168 | tf_op jit(solution)/shard_map/ppermute | solution.py:12
  133.5 10.5 %copy-start.28 = (s32[1024]{0:T(1024)S(1)}, s32[1024]{0:T(1024)}, u32[]{:S(2)}) copy-start(s32[1024]{0:T(1024)} %fusion.50) | copy-start | bytes 12292
  143.9 10.5 %copy-start.27 = (s32[1024]{0:T(1024)S(1)}, s32[1024]{0:T(1024)}, u32[]{:S(2)}) copy-start(s32[1024]{0:T(1024)} %fusion.51) | copy-start | bytes 12292
  154.4 10.5 %copy-start.26 = (s32[1024]{0:T(1024)S(1)}, s32[1024]{0:T(1024)}, u32[]{:S(2)}) copy-start(s32[1024]{0:T(1024)} %fusion.52) | copy-start | bytes 12292
  164.8 10.4 %copy-start.25 = (s32[1024]{0:T(1024)S(1)}, s32[1024]{0:T(1024)}, u32[]{:S(2)}) copy-start(s32[1024]{0:T(1024)} %fusion.53) | copy-start | bytes 12292
  175.3 10.4 %copy-start.24 = (s32[1024]{0:T(1024)S(1)}, s32[1024]{0:T(1024)}, u32[]{:S(2)}) copy-start(s32[1024]{0:T(1024)} %fusion.54) | copy-start | bytes 12292
  185.7 10.5 %copy-start.23 = (s32[1024]{0:T(1024)S(1)}, s32[1024]{0:T(1024)}, u32[]{:S(2)}) copy-start(s32[1024]{0:T(1024)} %fusion.55) | copy-start | bytes 12292
  196.2 10.5 %copy-start.22 = (s32[1024]{0:T(1024)S(1)}, s32[1024]{0:T(1024)}, u32[]{:S(2)}) copy-start(s32[1024]{0:T(1024)} %fusion.56) | copy-start | bytes 12292
  206.7 10.7 %copy-start.1 = (f32[20,3,2048]{2,0,1:T(8,128)S(1)}, f32[20,3,2048]{2,0,1:T(8,128)}, u32[]{:S(2)}) copy-start(f32[20,3,2048]{2,0,1:T(8,128)} %param.17) | copy-start | bytes 1474564
  206.7 10.7 %copy-start.55 = (pred[1024]{0:T(1024)(128)(4,1)S(1)}, pred[1024]{0:T(1024)(128)(4,1)}, u32[]{:S(2)}) copy-start(pred[1024]{0:T(1024)(128)(4,1)} %get-tuple-element.91) | copy-start | bytes 3076
  206.7 10.7 %copy-start.56 = (pred[1024]{0:T(1024)(128)(4,1)S(1)}, pred[1024]{0:T(1024)(128)(4,1)}, u32[]{:S(2)}) copy-start(pred[1024]{0:T(1024)(128)(4,1)} %get-tuple-element.92) | copy-start | bytes 3076
  217.4 9.0 %copy-start.53 = (s32[512]{0:T(512)S(1)}, s32[512]{0:T(512)}, u32[]{:S(2)}) copy-start(s32[512]{0:T(512)} %compare_select_fusion.17) | copy-start | bytes 6148
  218.8 9.8 %copy-start.46 = (s32[1024]{0:T(1024)S(1)}, s32[1024]{0:T(1024)}, u32[]{:S(2)}) copy-start(s32[1024]{0:T(1024)} %pad_clamp_fusion.17) | copy-start | bytes 12292
  219.3 11.7 %copy-start.45 = (s32[1024]{0:T(1024)S(1)}, s32[1024]{0:T(1024)}, u32[]{:S(2)}) copy-start(s32[1024]{0:T(1024)} %pad_clamp_fusion.16) | copy-start | bytes 12292
  220.2 7.2 %collective-permute-start.4 = (f32[20,3,64]{2,0,1:T(8,128)S(1)}, f32[20,3,64]{2,0,1:T(8,128)S(1)}, u32[]{:S(2)}, u32[]{:S(2)}) collective-permute-start(f32[20,3,64]{2,0,1:T(8,128)S(1)} %bitcast.337), channel_id=1, source_target_pairs={{28,0},{0,4},{4,8},{8,12},{12,16},{16,20},{20,24},{24,28},{29,1},{... | collective-permute-start | bytes 46088 | tf_op jit(solution)/shard_map/ppermute | solution.py:12
  221.3 6.7 %collective-permute-start.5 = (f32[20,3,64]{2,0,1:T(8,128)S(1)}, f32[20,3,64]{2,0,1:T(8,128)S(1)}, u32[]{:S(2)}, u32[]{:S(2)}) collective-permute-start(f32[20,3,64]{2,0,1:T(8,128)S(1)} %bitcast.339), channel_id=1, source_target_pairs={{4,0},{8,4},{12,8},{16,12},{20,16},{24,20},{28,24},{0,28},{5,1},{9... | collective-permute-start | bytes 46088 | tf_op jit(solution)/shard_map/ppermute | solution.py:12
  233.1 5.8 %copy-start.42 = (s32[1024]{0:T(1024)S(1)}, s32[1024]{0:T(1024)}, u32[]{:S(2)}) copy-start(s32[1024]{0:T(1024)} %pad_clamp_fusion.13) | copy-start | bytes 12292
  235.5 6.4 %copy-start.41 = (s32[1024]{0:T(1024)S(1)}, s32[1024]{0:T(1024)}, u32[]{:S(2)}) copy-start(s32[1024]{0:T(1024)} %pad_clamp_fusion.12) | copy-start | bytes 12292
  237.9 7.1 %copy-start.40 = (s32[1024]{0:T(1024)S(1)}, s32[1024]{0:T(1024)}, u32[]{:S(2)}) copy-start(s32[1024]{0:T(1024)} %pad_clamp_fusion.11) | copy-start | bytes 12292
  241.0 7.1 %copy-start.39 = (s32[1024]{0:T(1024)S(1)}, s32[1024]{0:T(1024)}, u32[]{:S(2)}) copy-start(s32[1024]{0:T(1024)} %pad_clamp_fusion.10) | copy-start | bytes 12292
  244.0 6.4 %copy-start.50 = (f32[1,512]{1,0:T(1,128)S(1)}, f32[1,512]{1,0:T(1,128)}, u32[]{:S(2)}) copy-start(f32[1,512]{1,0:T(1,128)} %get-tuple-element.55) | copy-start | bytes 6148
  244.0 6.4 %copy-start.51 = (f32[1,512]{1,0:T(1,128)S(1)}, f32[1,512]{1,0:T(1,128)}, u32[]{:S(2)}) copy-start(f32[1,512]{1,0:T(1,128)} %get-tuple-element.56) | copy-start | bytes 6148
  250.1 9.2 %copy-start.52 = (s32[512]{0:T(512)S(1)}, s32[512]{0:T(512)}, u32[]{:S(2)}) copy-start(s32[512]{0:T(512)} %compare_select_fusion.16) | copy-start | bytes 6148
  251.8 9.8 %copy-start.37 = (s32[1024]{0:T(1024)S(1)}, s32[1024]{0:T(1024)}, u32[]{:S(2)}) copy-start(s32[1024]{0:T(1024)} %pad_clamp_fusion.7) | copy-start | bytes 12292
  252.2 11.7 %copy-start.36 = (s32[1024]{0:T(1024)S(1)}, s32[1024]{0:T(1024)}, u32[]{:S(2)}) copy-start(s32[1024]{0:T(1024)} %pad_clamp_fusion.6) | copy-start | bytes 12292
  253.1 7.0 %collective-permute-start.6 = (f32[20,3,64]{2,0,1:T(8,128)S(1)}, f32[20,3,64]{2,0,1:T(8,128)S(1)}, u32[]{:S(2)}, u32[]{:S(2)}) collective-permute-start(f32[20,3,64]{2,0,1:T(8,128)S(1)} %bitcast.338), channel_id=1, source_target_pairs={{28,0},{0,4},{4,8},{8,12},{12,16},{16,20},{20,24},{24,28},{29,1},{... | collective-permute-start | bytes 46088 | tf_op jit(solution)/shard_map/ppermute | solution.py:12
  254.0 6.9 %collective-permute-start.7 = (f32[20,3,64]{2,0,1:T(8,128)S(1)}, f32[20,3,64]{2,0,1:T(8,128)S(1)}, u32[]{:S(2)}, u32[]{:S(2)}) collective-permute-start(f32[20,3,64]{2,0,1:T(8,128)S(1)} %bitcast.340), channel_id=1, source_target_pairs={{4,0},{8,4},{12,8},{16,12},{20,16},{24,20},{28,24},{0,28},{5,1},{9... | collective-permute-start | bytes 46088 | tf_op jit(solution)/shard_map/ppermute | solution.py:12
  273.9 7.1 %copy-start.47 = (s32[1024]{0:T(1024)S(1)}, s32[1024]{0:T(1024)}, u32[]{:S(2)}) copy-start(s32[1024]{0:T(1024)} %pad_clamp_fusion) | copy-start | bytes 12292
  276.9 6.4 %copy-start.48 = (f32[1,512]{1,0:T(1,128)S(1)}, f32[1,512]{1,0:T(1,128)}, u32[]{:S(2)}) copy-start(f32[1,512]{1,0:T(1,128)} %get-tuple-element.39) | copy-start | bytes 6148
  276.9 6.4 %copy-start.49 = (f32[1,512]{1,0:T(1,128)S(1)}, f32[1,512]{1,0:T(1,128)}, u32[]{:S(2)}) copy-start(f32[1,512]{1,0:T(1,128)} %get-tuple-element.40) | copy-start | bytes 6148
  293.2 11.9 %all-to-all-start = ((f32[4,1,30720]{2,1,0:T(1,128)}), f32[4,1,30720]{2,1,0:T(1,128)S(1)}, u32[]{:S(2)}, u32[]{:S(2)}) async-start(f32[4,1,30720]{2,1,0:T(1,128)} %reshape.717), calls=%async_computation | async-start | bytes 983040 | tf_op jit(solution)/shard_map/all_to_all | solution.py:88
  (35 other events, 96.9 us)
where the time goes:
time: 319 us; the launch traced here: 318 us
  local copies, waits for them, and re-layouts  243 us (76%)
  other arithmetic  34.1 us (11%)
  starting transfers between devices  25.3 us (8%)
  waiting for transfers between devices  12.4 us (4%)
    gather x64, local copies, waits for them, and re-layouts, weighted(): picked = jnp.take(extended, links[neighbour], axis=2)  209 us
    ppermute x8, starting transfers between devices, passed_along(): return lax.ppermute(block, axis, route)  21.6 us
    gather x32, other arithmetic  13.7 us
    unnamed x150, local copies, waits for them, and re-layouts  10.7 us
    and x16, other arithmetic, weighted(): picked = jnp.take(extended, links[neighbour], axis=2)  9.21 us
    all_to_all x1, waiting for transfers between devices, on_device(): lax.all_to_all(bands, 'lev', split_axis=2, concat_axis=0, tiled=True)  8.15 us
  transfers between devices with their start and end apart: 9, of which 7 were waited for; matrix products, arithmetic and copies ran while one was open for 10% of the time, Pallas kernels for 0%

commit v1 on v0

v1 whole, which is shorter than its diff:
```python
import functools

import jax
import jax.numpy as jnp
import ml_dtypes
import numpy as np
from jax import lax
from jax.experimental import pallas as pl
from jax.experimental.pallas import tpu as pltpu
from jax.sharding import PartitionSpec as P

LANES = 128
SUB = 8
MESH = pl.DeviceIdType.MESH


def cosine_table(length):
    rows = np.arange(length, dtype=np.float64)[:, None]
    columns = np.arange(length, dtype=np.float64)[None, :]
    matrix = np.cos(np.pi * (columns + 0.5) * rows / length) * np.sqrt(2.0 / length)
    matrix[0] *= np.sqrt(0.5)
    return matrix


def spread_table(levels, tracers, groups, padded):
    own = levels // groups
    table = cosine_table(levels).reshape(levels, groups, own)
    wide = np.zeros((tracers, levels, groups, padded))
    for t in range(tracers):
        wide[t, :, :, t * own : (t + 1) * own] = table
    wide = wide.reshape(levels * tracers, groups * padded).astype(np.float32)
    high = wide.astype(ml_dtypes.bfloat16)
    low = (wide - high.astype(np.float32)).astype(ml_dtypes.bfloat16)
    return high, low


def halves(x):
    high = x.astype(jnp.bfloat16)
    low = (x - high.astype(jnp.float32)).astype(jnp.bfloat16)
    return high, low


def build(links, weights, merged, w_high, w_low, first, count, blocks):
    slots = links.shape[0]
    groups = -(-blocks // SUB)

    def column(tile, _):
        cols = pl.ds(pl.multiple_of(first + tile * LANES, LANES), LANES)
        lane = []
        block = []
        weight = []
        for k in range(slots):
            link = jnp.broadcast_to(links[k : k + 1, cols], (SUB, LANES))
            lane.append(link & (LANES - 1))
            block.append(link >> 7)
            weight.append(jnp.broadcast_to(weights[k : k + 1, cols], (SUB, LANES)))
        which = lax.broadcasted_iota(jnp.int32, (SUB, LANES), 0)
        for g in range(groups):
            placed = []
            for k in range(slots):
                mine = jnp.where(block[k] == which + g * SUB, weight[k], 0.0)
                total = mine
                for j in range(k):
                    total = total + jnp.where(lane[j] == lane[k], placed[j], 0.0)
                placed.append(mine)
                merged[k, g * SUB : (g + 1) * SUB, :] = total
        lane2 = [jnp.concatenate([v, v], axis=0) for v in lane]

        def strip(s, _):
            rows16 = lax.broadcasted_iota(jnp.int32, (2 * SUB, LANES), 0) + s * (2 * SUB)
            masks = [lane2[k] == rows16 for k in range(slots)]
            for b in range(blocks):
                total = jnp.zeros((2 * SUB, LANES), jnp.float32)
                for k in range(slots):
                    row = jnp.broadcast_to(merged[k, b : b + 1, :], (2 * SUB, LANES))
                    total = jnp.where(masks[k], row, total)
                high, low = halves(total)
                place = pl.ds(pl.multiple_of(b * LANES + s * (2 * SUB), 2 * SUB), 2 * SUB)
                w_high[place, cols] = high
                w_low[place, cols] = low
            return 0

        lax.fori_loop(0, LANES // (2 * SUB), strip, 0)
        return 0

    lax.fori_loop(0, count // LANES, column, 0)


def picked(source, start, blocks, index, out):
    lane = jnp.broadcast_to(index & (LANES - 1), (SUB, LANES))
    block = jnp.broadcast_to(index >> 7, (SUB, LANES))
    for r in range(source.shape[0] // SUB):
        rows = slice(r * SUB, (r + 1) * SUB)
        got = None
        for b in range(blocks):
            cols = slice(start + b * LANES, start + (b + 1) * LANES)
            t = jnp.take_along_axis(source[rows, cols], lane, axis=1)
            got = t if got is None else jnp.where(block == b, t, got)
        out[rows, :] = got


def put(ext, padded, at, value):
    high, low = halves(value)
    width = value.shape[1]
    ext[0:padded, at : at + width] = high
    ext[padded : 2 * padded, at : at + width] = low


def product(ext, padded, depth, w_high, w_low, cols):
    both = jnp.dot(ext[:, 0:depth], w_high[:, cols], preferred_element_type=jnp.float32)
    rest = jnp.dot(ext[0:padded, 0:depth], w_low[:, cols], preferred_element_type=jnp.float32)
    return both[0:padded] + both[padded : 2 * padded] + rest


def body(
    n_patch, n_lev, levels,
    field, sc1, sd1, sc2, sd2, pl1, pw1, ul1, uw1, pl2, pw2, ul2, uw2, t_high, t_low,
    out,
    xs, ext, merged, p1h, p1l, u1h, u1l, p2h, p2l, u2h, u2l,
    det1, sm1, det2, sm2, hsend, hrecv, gathered, res,
    hs_sem, hr_sem, as_sem, ar_sem,
):
    tracers, own, cells = field.shape
    rows = own * tracers
    padded = xs.shape[0]
    n1 = cells // 2
    n2 = cells // 4
    halo1 = sc1.shape[2]
    halo2 = sc2.shape[2]
    chunk = cells // n_lev
    me = lax.axis_index("lev")
    patch = lax.axis_index("patch")
    left = lax.rem(patch + n_patch - 1, n_patch)
    right = lax.rem(patch + 1, n_patch)

    barrier = pltpu.get_barrier_semaphore()
    for neighbour in (left, right):
        pl.semaphore_signal(barrier, inc=1, device_id={"patch": neighbour}, device_id_type=MESH)
    for d in range(1, n_lev):
        pl.semaphore_signal(
            barrier, inc=1, device_id={"lev": lax.rem(me + d, n_lev)}, device_id_type=MESH
        )

    if padded > rows:
        edge = rows // SUB * SUB
        xs[edge:padded, :] = jnp.zeros((padded - edge, cells), jnp.float32)
    for t in range(tracers):
        xs[t * own : (t + 1) * own, :] = field[t]

    def swap(phase, first_buf, second_buf):
        copies = []
        for side, (buf, to) in enumerate(((second_buf, right), (first_buf, left))):
            copies.append(
                pltpu.make_async_remote_copy(
                    src_ref=buf,
                    dst_ref=hrecv.at[phase, side],
                    send_sem=hs_sem.at[phase, side],
                    recv_sem=hr_sem.at[phase, side],
                    device_id={"patch": to},
                    device_id_type=MESH,
                )
            )
        for c in copies:
            c.start()
        return copies

    def send_one(phase, source, start, blocks, send):
        picked(source, start, blocks, send[0, 0:1, :], hsend.at[phase, 0])
        picked(source, start, blocks, send[0, 1:2, :], hsend.at[phase, 1])

    def send_two(phase, source, start, blocks, send):
        index = jnp.concatenate([send[0, 1:2, :], send[0, 0:1, :]], axis=1)
        picked(source, start, blocks, index, hsend.at[phase, 0])

    def land_one(phase, at):
        put(ext, padded, at, hrecv[phase, 0])
        put(ext, padded, at + halo1, hrecv[phase, 1])

    def land_two(phase, at):
        lanes = lax.broadcasted_iota(jnp.int32, (padded, LANES), 1)
        put(ext, padded, at, jnp.where(lanes < halo2, hrecv[phase, 0], hrecv[phase, 1]))

    outgoing = []

    def scatter(source, base):
        for piece in range(source.shape[1] // chunk):
            d = base // chunk + piece
            part = source.at[:, piece * chunk : (piece + 1) * chunk]
            copy = pltpu.make_async_remote_copy(
                src_ref=part,
                dst_ref=gathered.at[me],
                send_sem=as_sem.at[d],
                recv_sem=ar_sem.at[me],
                device_id={"lev": d},
                device_id_type=MESH,
            )
            outgoing.append((d, copy))

            @pl.when(me != d)
            def _():
                copy.start()

            @pl.when(me == d)
            def _():
                gathered[d] = part[...]

    b1 = n1 // LANES
    b2 = n2 // LANES
    e1 = n1 + 2 * halo1
    e2 = n2 + 2 * halo2
    wide = 256

    send_one(0, xs, n1, b1, sc1)
    pl.semaphore_wait(barrier, 2 + n_lev - 1)
    flight = swap(0, hsend.at[0, 0], hsend.at[0, 1])
    put(ext, padded, 0, xs[:, n1:cells])
    build(pl1, pw1, merged, p1h, p1l, 0, n1, e1 // LANES)
    for c in flight:
        c.wait()
    land_one(0, n1)
    for c in range(0, n1, wide):
        cols = slice(c, c + wide)
        det1[:, cols] = xs[:, cols] - product(ext, padded, e1, p1h, p1l, cols)

    send_one(1, det1, 0, b1, sd1)
    flight = swap(1, hsend.at[1, 0], hsend.at[1, 1])
    scatter(det1, 0)
    put(ext, padded, 0, det1[...])
    build(ul1, uw1, merged, u1h, u1l, n2, n2, e1 // LANES)
    build(pl2, pw2, merged, p2h, p2l, 0, n2, e2 // LANES)
    for c in flight:
        c.wait()
    land_one(1, n1)
    for c in range(n2, n1, wide):
        cols = slice(c, c + wide)
        sm1[:, cols] = xs[:, n1 + c : n1 + c + wide] + product(ext, padded, e1, u1h, u1l, cols)

    send_two(2, sm1, n2, b2, sc2)
    flight = swap(2, hsend.at[2, 0], hsend.at[2, 0])
    build(ul1, uw1, merged, u1h, u1l, 0, n2, e1 // LANES)
    for c in range(0, n2, wide):
        cols = slice(c, c + wide)
        sm1[:, cols] = xs[:, n1 + c : n1 + c + wide] + product(ext, padded, e1, u1h, u1l, cols)
    put(ext, padded, 0, sm1[:, n2:n1])
    for c in flight:
        c.wait()
    land_two(2, n2)
    for c in range(0, n2, wide):
        cols = slice(c, c + wide)
        det2[:, cols] = sm1[:, cols] - product(ext, padded, e2, p2h, p2l, cols)

    send_two(3, det2, 0, b2, sd2)
    flight = swap(3, hsend.at[3, 0], hsend.at[3, 0])
    scatter(det2, n1)
    put(ext, padded, 0, det2[...])
    build(ul2, uw2, merged, u2h, u2l, 0, n2, e2 // LANES)
    for c in flight:
        c.wait()
    land_two(3, n2)
    for c in range(0, n2, wide):
        cols = slice(c, c + wide)
        sm2[:, cols] = sm1[:, n2 + c : n2 + c + wide] + product(ext, padded, e2, u2h, u2l, cols)
    scatter(sm2, n1 + n2)

    for s in range(n_lev):

        @pl.when(me != s)
        def _():
            pltpu.make_async_remote_copy(
                src_ref=gathered.at[s],
                dst_ref=gathered.at[s],
                send_sem=as_sem.at[s],
                recv_sem=ar_sem.at[s],
                device_id={"lev": s},
                device_id_type=MESH,
            ).wait_recv()

    high, low = halves(gathered[...].reshape(n_lev * padded, chunk))
    res[...] = (
        jnp.dot(t_high[...], high, preferred_element_type=jnp.float32)
        + jnp.dot(t_high[...], low, preferred_element_type=jnp.float32)
        + jnp.dot(t_low[...], high, preferred_element_type=jnp.float32)
    )
    for t in range(tracers):
        out[t] = res[t * levels : (t + 1) * levels, :]

    for d, copy in outgoing:

        @pl.when(me != d)
        def _():
            copy.wait_send()


def on_device(n_patch, n_lev, *args):
    field, sc1 = args[0], args[1]
    own, tracers, cells = field.shape
    levels = own * n_lev
    rows = own * tracers
    padded = -(-rows // (2 * SUB)) * (2 * SUB)
    n1, n2 = cells // 2, cells // 4
    e1 = n1 + 2 * sc1.shape[2]
    e2 = n2 + 2 * args[3].shape[2]
    chunk = cells // n_lev
    slots = args[5].shape[0]
    t_high, t_low = spread_table(levels, tracers, n_lev, padded)
    f32, bf16 = jnp.float32, jnp.bfloat16
    result = pl.pallas_call(
        functools.partial(body, n_patch, n_lev, levels),
        out_shape=jax.ShapeDtypeStruct((tracers, levels, chunk), f32),
        in_specs=[pl.BlockSpec(memory_space=pltpu.VMEM)] * 15,
        out_specs=pl.BlockSpec(memory_space=pltpu.VMEM),
        scratch_shapes=[
            pltpu.VMEM((padded, cells), f32),
            pltpu.VMEM((2 * padded, e1), bf16),
            pltpu.VMEM((slots, -(-(e1 // LANES) // SUB) * SUB, LANES), f32),
            pltpu.VMEM((e1, n1), bf16),
            pltpu.VMEM((e1, n1), bf16),
            pltpu.VMEM((e1, n1), bf16),
            pltpu.VMEM((e1, n1), bf16),
            pltpu.VMEM((e2, n2), bf16),
            pltpu.VMEM((e2, n2), bf16),
            pltpu.VMEM((e2, n2), bf16),
            pltpu.VMEM((e2, n2), bf16),
            pltpu.VMEM((padded, n1), f32),
            pltpu.VMEM((padded, n1), f32),
            pltpu.VMEM((padded, n2), f32),
            pltpu.VMEM((padded, n2), f32),
            pltpu.VMEM((4, 2, padded, LANES), f32),
            pltpu.VMEM((4, 2, padded, LANES), f32),
            pltpu.VMEM((n_lev, padded, chunk), f32),
            pltpu.VMEM((levels * tracers, chunk), f32),
            pltpu.SemaphoreType.DMA((4, 2)),
            pltpu.SemaphoreType.DMA((4, 2)),
            pltpu.SemaphoreType.DMA((n_lev,)),
            pltpu.SemaphoreType.DMA((n_lev,)),
        ],
        compiler_params=pltpu.CompilerParams(collective_id=0, has_side_effects=True),
    )(jnp.transpose(field, (1, 0, 2)), *args[1:], jnp.asarray(t_high), jnp.asarray(t_low))
    return jnp.transpose(result, (1, 0, 2))


def solution(mesh):
    in_specs = (P("lev", None, "patch"),)
    in_specs += (P("patch", None, None),) * 4
    in_specs += (P(None, "patch"),) * 8
    out_specs = P(None, None, ("patch", "lev"))
    fn = functools.partial(on_device, mesh.shape["patch"], mesh.shape["lev"])
    return jax.shard_map(
        fn, mesh=mesh, in_specs=in_specs, out_specs=out_specs, check_vma=False
    )
```

time: 319 us -> 32.4 us (0.10)
  local copies, waits for them, and re-layouts: 243 us -> 1.84 us
  other arithmetic: 34.1 us -> 0 us
  Pallas kernels: 0 us -> 30.3 us
  starting transfers between devices: 25.3 us -> 0 us
  waiting for transfers between devices: 12.4 us -> 0 us
    gather x80 -> x0, local copies, waits for them, and re-layouts: 217 us -> none  [the longest x64 209 us: weighted(): picked = jnp.take(extended, links[neighbour], axis=2)]
    pallas_call x0 -> x1, Pallas kernels: none -> 30.3 us  [on_device(): pl.pallas_call(functools.partial(body, n_patch, n_lev, levels), out_shape...]
    ppermute x8 -> x0, starting transfers between devices: 21.6 us -> none  [passed_along(): return lax.ppermute(block, axis, route)]
    gather x36 -> x0, other arithmetic: 15.5 us -> none
    and x16 -> x0, other arithmetic: 9.21 us -> none  [weighted(): picked = jnp.take(extended, links[neighbour], axis=2)]
    unnamed x150 -> x1, local copies, waits for them, and re-layouts: 10.7 us -> 1.84 us
    all_to_all x1 -> x0, waiting for transfers between devices: 8.15 us -> none  [on_device(): lax.all_to_all(bands, 'lev', split_axis=2, concat_axis=0, tiled=True)]
    concatenate x5 -> x0, local copies, waits for them, and re-layouts: 6.25 us -> none  [the longest x1 3.12 us: on_device(): bands = jnp.concatenate([detail1, detail2, smooth2], axis=2)]
  transfers between devices with their start and end apart: 9 -> 0, of which waited for: 7 -> 0; matrix products, arithmetic and copies ran while one was open for 10% -> 0% of each run, Pallas kernels for 0% -> 0%
where the time goes in v1:
time: 32.4 us; the launch traced here: 32.2 us
  Pallas kernels  30.3 us (94%)
  local copies, waits for them, and re-layouts  1.84 us (6%)
    pallas_call x1, Pallas kernels, on_device(): pl.pallas_call(functools.partial(body, n_patch, n_lev, levels), out_shape...  30.3 us
    unnamed x1, local copies, waits for them, and re-layouts  1.84 us

profile of v1, /device:TPU:0, one launch (start us, length us, event | category | flops | bytes accessed | tf_op | source)
XLA Modules:
  0.0 32.2 jit_solution(1668273267562066934)
XLA Ops:
  0.0 30.3 %shard_map.145 = f32[3,80,512]{2,1,0:T(8,128)} custom-call(f32[3,20,2048]{2,1,0:T(8,128)} %bitcast.3, s32[1,2,128]{2,1,0:T(2,128)} %sc1.1, s32[1,2,128]{2,1,0:T(2,128)} %sd1.1, s32[1,2,64]{2,1,0:T(2,128)} %sc2.1, s32[1,2,64]{2,1,0:T(2,128)} %sd2.1, s32[8,1024]{1,0:T(8,128)} %pl1.1, f32[8,1024]{1,0:T(8,128)} %pw1.1, s32[8,1024]{1,0:T(8,128)} %ul1.1, ...), custom_call_target="tpu_custom_call" | custom-call | tf_op jit(solution)/shard_map/pallas_call | solution.py:307
  30.3 1.8 %copy.17 = f32[80,3,512]{2,0,1:T(8,128)} copy(f32[80,3,512]{2,0,1:T(8,128)} %bitcast.2) | data formatting | bytes 983040

commit v2 on v1

--- a/solution.py
+++ b/solution.py
@@ -106,18 +106,19 @@
     ext[padded : 2 * padded, at : at + width] = low
 
 
-def product(ext, padded, depth, w_high, w_low, cols):
-    both = jnp.dot(ext[:, 0:depth], w_high[:, cols], preferred_element_type=jnp.float32)
-    rest = jnp.dot(ext[0:padded, 0:depth], w_low[:, cols], preferred_element_type=jnp.float32)
+def product(ext, padded, span, w_high, w_low, cols):
+    k = slice(*span)
+    both = jnp.dot(ext[:, k], w_high[k, cols], preferred_element_type=jnp.float32)
+    rest = jnp.dot(ext[0:padded, k], w_low[k, cols], preferred_element_type=jnp.float32)
     return both[0:padded] + both[padded : 2 * padded] + rest
 
 
 def body(
     n_patch, n_lev, levels,
-    field, sc1, sd1, sc2, sd2, pl1, pw1, ul1, uw1, pl2, pw2, ul2, uw2, t_high, t_low,
-    out,
+    field, sc1, sd1, sc2, sd2, pl1, pw1, ul1, uw1, pl2, pw2, ul2, uw2,
+    gathered,
     xs, ext, merged, p1h, p1l, u1h, u1l, p2h, p2l, u2h, u2l,
-    det1, sm1, det2, sm2, hsend, hrecv, gathered, res,
+    det1, sm1, det2, sm2, hsend, hrecv,
     hs_sem, hr_sem, as_sem, ar_sem,
 ):
     tracers, own, cells = field.shape
@@ -210,56 +211,72 @@
     e2 = n2 + 2 * halo2
     wide = 256
 
+    def predict(into, start, values, depth, w_high, w_low, n, add):
+        for c in range(0, n, wide):
+            cols = slice(start + c, start + c + wide)
+            got = product(ext, padded, depth, w_high, w_low, cols)
+            old = values(cols)
+            into[:, cols] = old + got if add else old - got
+
+    def fine1(cols):
+        return xs[:, cols]
+
+    def coarse1(cols):
+        return xs[:, n1 + cols.start : n1 + cols.stop]
+
+    def fine2(cols):
+        return sm1[:, cols]
+
+    def coarse2(cols):
+        return sm1[:, n2 + cols.start : n2 + cols.stop]
+
+    def held(ref):
+        return lambda cols: ref[:, cols]
+
     send_one(0, xs, n1, b1, sc1)
     pl.semaphore_wait(barrier, 2 + n_lev - 1)
     flight = swap(0, hsend.at[0, 0], hsend.at[0, 1])
     put(ext, padded, 0, xs[:, n1:cells])
     build(pl1, pw1, merged, p1h, p1l, 0, n1, e1 // LANES)
+    predict(det1, 0, fine1, (0, n1), p1h, p1l, n1, False)
     for c in flight:
         c.wait()
     land_one(0, n1)
-    for c in range(0, n1, wide):
-        cols = slice(c, c + wide)
-        det1[:, cols] = xs[:, cols] - product(ext, padded, e1, p1h, p1l, cols)
+    predict(det1, 0, held(det1), (n1, e1), p1h, p1l, n1, False)
 
     send_one(1, det1, 0, b1, sd1)
     flight = swap(1, hsend.at[1, 0], hsend.at[1, 1])
     scatter(det1, 0)
     put(ext, padded, 0, det1[...])
     build(ul1, uw1, merged, u1h, u1l, n2, n2, e1 // LANES)
+    predict(sm1, n2, coarse1, (0, n1), u1h, u1l, n2, True)
     build(pl2, pw2, merged, p2h, p2l, 0, n2, e2 // LANES)
     for c in flight:
         c.wait()
     land_one(1, n1)
-    for c in range(n2, n1, wide):
-        cols = slice(c, c + wide)
-        sm1[:, cols] = xs[:, n1 + c : n1 + c + wide] + product(ext, padded, e1, u1h, u1l, cols)
+    predict(sm1, n2, held(sm1), (n1, e1), u1h, u1l, n2, True)
 
     send_two(2, sm1, n2, b2, sc2)
     flight = swap(2, hsend.at[2, 0], hsend.at[2, 0])
     build(ul1, uw1, merged, u1h, u1l, 0, n2, e1 // LANES)
-    for c in range(0, n2, wide):
-        cols = slice(c, c + wide)
-        sm1[:, cols] = xs[:, n1 + c : n1 + c + wide] + product(ext, padded, e1, u1h, u1l, cols)
+    predict(sm1, 0, coarse1, (0, e1), u1h, u1l, n2, True)
     put(ext, padded, 0, sm1[:, n2:n1])
+    predict(det2, 0, fine2, (0, n2), p2h, p2l, n2, False)
     for c in flight:
         c.wait()
     land_two(2, n2)
-    for c in range(0, n2, wide):
-        cols = slice(c, c + wide)
-        det2[:, cols] = sm1[:, cols] - product(ext, padded, e2, p2h, p2l, cols)
+    predict(det2, 0, held(det2), (n2, e2), p2h, p2l, n2, False)
 
     send_two(3, det2, 0, b2, sd2)
     flight = swap(3, hsend.at[3, 0], hsend.at[3, 0])
     scatter(det2, n1)
     put(ext, padded, 0, det2[...])
     build(ul2, uw2, merged, u2h, u2l, 0, n2, e2 // LANES)
+    predict(sm2, 0, coarse2, (0, n2), u2h, u2l, n2, True)
     for c in flight:
         c.wait()
     land_two(3, n2)
-    for c in range(0, n2, wide):
-        cols = slice(c, c + wide)
-        sm2[:, cols] = sm1[:, n2 + c : n2 + c + wide] + product(ext, padded, e2, u2h, u2l, cols)
+    predict(sm2, 0, held(sm2), (n2, e2), u2h, u2l, n2, True)
     scatter(sm2, n1 + n2)
 
     for s in range(n_lev):
@@ -275,20 +292,24 @@
                 device_id_type=MESH,
             ).wait_recv()
 
-    high, low = halves(gathered[...].reshape(n_lev * padded, chunk))
-    res[...] = (
-        jnp.dot(t_high[...], high, preferred_element_type=jnp.float32)
-        + jnp.dot(t_high[...], low, preferred_element_type=jnp.float32)
-        + jnp.dot(t_low[...], high, preferred_element_type=jnp.float32)
-    )
-    for t in range(tracers):
-        out[t] = res[t * levels : (t + 1) * levels, :]
-
     for d, copy in outgoing:
 
         @pl.when(me != d)
         def _():
             copy.wait_send()
+
+
+def transform(gathered, t_high, t_low, out):
+    groups, padded, chunk = gathered.shape
+    tracers, levels, _ = out.shape
+    high, low = halves(gathered[...].reshape(groups * padded, chunk))
+    for t in range(tracers):
+        rows = slice(t * levels, (t + 1) * levels)
+        out[t] = (
+            jnp.dot(t_high[rows, :], high, preferred_element_type=jnp.float32)
+            + jnp.dot(t_high[rows, :], low, preferred_element_type=jnp.float32)
+            + jnp.dot(t_low[rows, :], high, preferred_element_type=jnp.float32)
+        )
 
 
 def on_device(n_patch, n_lev, *args):
@@ -304,10 +325,10 @@
     slots = args[5].shape[0]
     t_high, t_low = spread_table(levels, tracers, n_lev, padded)
     f32, bf16 = jnp.float32, jnp.bfloat16
-    result = pl.pallas_call(
+    gathered = pl.pallas_call(
         functools.partial(body, n_patch, n_lev, levels),
-        out_shape=jax.ShapeDtypeStruct((tracers, levels, chunk), f32),
-        in_specs=[pl.BlockSpec(memory_space=pltpu.VMEM)] * 15,
+        out_shape=jax.ShapeDtypeStruct((n_lev, padded, chunk), f32),
+        in_specs=[pl.BlockSpec(memory_space=pltpu.VMEM)] * 13,
         out_specs=pl.BlockSpec(memory_space=pltpu.VMEM),
         scratch_shapes=[
             pltpu.VMEM((padded, cells), f32),
@@ -327,15 +348,19 @@
             pltpu.VMEM((padded, n2), f32),
             pltpu.VMEM((4, 2, padded, LANES), f32),
             pltpu.VMEM((4, 2, padded, LANES), f32),
-            pltpu.VMEM((n_lev, padded, chunk), f32),
-            pltpu.VMEM((levels * tracers, chunk), f32),
             pltpu.SemaphoreType.DMA((4, 2)),
             pltpu.SemaphoreType.DMA((4, 2)),
             pltpu.SemaphoreType.DMA((n_lev,)),
             pltpu.SemaphoreType.DMA((n_lev,)),
         ],
         compiler_params=pltpu.CompilerParams(collective_id=0, has_side_effects=True),
-    )(jnp.transpose(field, (1, 0, 2)), *args[1:], jnp.asarray(t_high), jnp.asarray(t_low))
+    )(jnp.transpose(field, (1, 0, 2)), *args[1:])
+    result = pl.pallas_call(
+        transform,
+        out_shape=jax.ShapeDtypeStruct((tracers, levels, chunk), f32),
+        in_specs=[pl.BlockSpec(memory_space=pltpu.VMEM)] * 3,
+        out_specs=pl.BlockSpec(memory_space=pltpu.VMEM),
+    )(gathered, jnp.asarray(t_high), jnp.asarray(t_low))
     return jnp.transpose(result, (1, 0, 2))
 
 

time: 32.4 us -> 31.6 us (0.975)
  local copies, waits for them, and re-layouts: 1.84 us -> 0 us
  Pallas kernels: 30.3 us -> 31.5 us
    pallas_call x0 -> x1, Pallas kernels: none -> 2.47 us  [on_device(): pl.pallas_call(transform, out_shape=jax.ShapeDtypeStruct((tracers, levels...]
    unnamed x1 -> x0, local copies, waits for them, and re-layouts: 1.84 us -> none
    pallas_call x1, Pallas kernels: 30.3 us -> 29 us  [on_device(): pl.pallas_call(functools.partial(body, n_patch, n_lev, levels), out_shape...]
where the time goes in v2:
time: 31.6 us; the launch traced here: 31.5 us
  Pallas kernels  31.5 us (100%)
    pallas_call x1, Pallas kernels, on_device(): pl.pallas_call(functools.partial(body, n_patch, n_lev, levels), out_shape...  29 us
    pallas_call x1, Pallas kernels, on_device(): pl.pallas_call(transform, out_shape=jax.ShapeDtypeStruct((tracers, levels...  2.47 us

profile of v2, /device:TPU:0, one launch (start us, length us, event | category | flops | bytes accessed | tf_op | source)
XLA Modules:
  0.0 31.5 jit_solution(7741265327892462764)
XLA Ops:
  0.0 29.0 %shard_map.145.gathered = f32[4,64,512]{2,1,0:T(8,128)} custom-call(f32[3,20,2048]{2,1,0:T(8,128)} %bitcast.2, s32[1,2,128]{2,1,0:T(2,128)} %sc1.1, s32[1,2,128]{2,1,0:T(2,128)} %sd1.1, s32[1,2,64]{2,1,0:T(2,128)} %sc2.1, s32[1,2,64]{2,1,0:T(2,128)} %sd2.1, s32[8,1024]{1,0:T(8,128)} %pl1.1, f32[8,1024]{1,0:T(8,128)} %pw1.1, s32[8,1024]{1,0:T(8,128)} %ul1.1, ...), custom_call_target="tpu_custom_call" | custom-call | tf_op jit(solution)/shard_map/pallas_call | solution.py:328
  29.0 2.5 %shard_map.146 = f32[3,80,512]{2,1,0:T(8,128)} custom-call(f32[4,64,512]{2,1,0:T(8,128)} %shard_map.145.gathered, bf16[240,256]{1,0:T(8,128)(2,1)} %constant.4.clone.t_high, bf16[240,256]{1,0:T(8,128)(2,1)} %constant.5.clone.t_low), custom_call_target="tpu_custom_call" | custom-call | tf_op jit(solution)/shard_map/pallas_call | solution.py:358

commit v3 on v2

--- a/solution.py
+++ b/solution.py
@@ -40,19 +40,20 @@
     return high, low
 
 
-def build(links, weights, merged, w_high, w_low, first, count, blocks):
+def build(links, weights, merged, w_high, w_low, first, count, blocks, base=0, shift=0):
     slots = links.shape[0]
     groups = -(-blocks // SUB)
 
     def column(tile, _):
         cols = pl.ds(pl.multiple_of(first + tile * LANES, LANES), LANES)
+        into = pl.ds(pl.multiple_of(first + shift + tile * LANES, LANES), LANES)
         lane = []
         block = []
         weight = []
         for k in range(slots):
             link = jnp.broadcast_to(links[k : k + 1, cols], (SUB, LANES))
             lane.append(link & (LANES - 1))
-            block.append(link >> 7)
+            block.append((link >> 7) - base)
             weight.append(jnp.broadcast_to(weights[k : k + 1, cols], (SUB, LANES)))
         which = lax.broadcasted_iota(jnp.int32, (SUB, LANES), 0)
         for g in range(groups):
@@ -76,8 +77,8 @@
                     total = jnp.where(masks[k], row, total)
                 high, low = halves(total)
                 place = pl.ds(pl.multiple_of(b * LANES + s * (2 * SUB), 2 * SUB), 2 * SUB)
-                w_high[place, cols] = high
-                w_low[place, cols] = low
+                w_high[place, into] = high
+                w_low[place, into] = low
             return 0
 
         lax.fori_loop(0, LANES // (2 * SUB), strip, 0)
@@ -113,12 +114,23 @@
     return both[0:padded] + both[padded : 2 * padded] + rest
 
 
+def small(value, m_high, m_low):
+    padded = value.shape[0]
+    high, low = halves(value)
+    both = jnp.concatenate([high, low], axis=0)
+    both = jnp.dot(both, m_high, preferred_element_type=jnp.float32)
+    rest = jnp.dot(high, m_low, preferred_element_type=jnp.float32)
+    return both[0:padded] + both[padded : 2 * padded] + rest
+
+
 def body(
     n_patch, n_lev, levels,
     field, sc1, sd1, sc2, sd2, pl1, pw1, ul1, uw1, pl2, pw2, ul2, uw2,
     gathered,
     xs, ext, merged, p1h, p1l, u1h, u1l, p2h, p2l, u2h, u2l,
     det1, sm1, det2, sm2, hsend, hrecv,
+    ext2, glink, gweight, rlink, rweight, mh, ml, part, full1, full2, done,
+    ms_sem, mr_sem,
     hs_sem, hr_sem, as_sem, ar_sem,
 ):
     tracers, own, cells = field.shape
@@ -148,38 +160,39 @@
     for t in range(tracers):
         xs[t * own : (t + 1) * own, :] = field[t]
 
-    def swap(phase, first_buf, second_buf):
-        copies = []
-        for side, (buf, to) in enumerate(((second_buf, right), (first_buf, left))):
-            copies.append(
-                pltpu.make_async_remote_copy(
-                    src_ref=buf,
-                    dst_ref=hrecv.at[phase, side],
-                    send_sem=hs_sem.at[phase, side],
-                    recv_sem=hr_sem.at[phase, side],
-                    device_id={"patch": to},
-                    device_id_type=MESH,
-                )
+    def copy_to(phase, side):
+        return pltpu.make_async_remote_copy(
+            src_ref=hsend.at[phase, side],
+            dst_ref=hrecv.at[phase, side],
+            send_sem=hs_sem.at[phase, side],
+            recv_sem=hr_sem.at[phase, side],
+            device_id={"patch": left if side else right},
+            device_id_type=MESH,
+        )
+
+    def meta_to(side):
+        return [
+            pltpu.make_async_remote_copy(
+                src_ref=mine.at[side],
+                dst_ref=theirs.at[side],
+                send_sem=ms_sem.at[which, side],
+                recv_sem=mr_sem.at[which, side],
+                device_id={"patch": left if side else right},
+                device_id_type=MESH,
             )
-        for c in copies:
-            c.start()
-        return copies
-
-    def send_one(phase, source, start, blocks, send):
-        picked(source, start, blocks, send[0, 0:1, :], hsend.at[phase, 0])
-        picked(source, start, blocks, send[0, 1:2, :], hsend.at[phase, 1])
-
-    def send_two(phase, source, start, blocks, send):
-        index = jnp.concatenate([send[0, 1:2, :], send[0, 0:1, :]], axis=1)
-        picked(source, start, blocks, index, hsend.at[phase, 0])
-
-    def land_one(phase, at):
-        put(ext, padded, at, hrecv[phase, 0])
-        put(ext, padded, at + halo1, hrecv[phase, 1])
-
-    def land_two(phase, at):
-        lanes = lax.broadcasted_iota(jnp.int32, (padded, LANES), 1)
-        put(ext, padded, at, jnp.where(lanes < halo2, hrecv[phase, 0], hrecv[phase, 1]))
+            for which, (mine, theirs) in enumerate(((glink, rlink), (gweight, rweight)))
+        ]
+
+    def both_sides(step):
+        @pl.when(patch == 0)
+        def _():
+            step(1)
+            step(0)
+
+        @pl.when(patch != 0)
+        def _():
+            step(0)
+            step(1)
 
     outgoing = []
 
@@ -214,7 +227,8 @@
     def predict(into, start, values, depth, w_high, w_low, n, add):
         for c in range(0, n, wide):
             cols = slice(start + c, start + c + wide)
-            got = product(ext, padded, depth, w_high, w_low, cols)
+            source = ext if n1 <= w_high.shape[1] else ext2
+            got = product(source, padded, depth, w_high, w_low, cols)
             old = values(cols)
             into[:, cols] = old + got if add else old - got
 
@@ -233,49 +247,130 @@
     def held(ref):
         return lambda cols: ref[:, cols]
 
-    send_one(0, xs, n1, b1, sc1)
-    pl.semaphore_wait(barrier, 2 + n_lev - 1)
-    flight = swap(0, hsend.at[0, 0], hsend.at[0, 1])
+    h1 = 2 * halo1 // LANES
+    h2 = 2 * halo2 // LANES
+    lower = lax.broadcasted_iota(jnp.int32, (padded, LANES), 1) < halo2
+
+    def tail(phase, side):
+        if phase == 2:
+            return slice(0, LANES)
+        return slice(side * LANES, (side + 1) * LANES)
+
+    def sided(phase, side, value):
+        if phase != 2:
+            return value
+        return jnp.where(lower, value, 0.0) if side == 0 else jnp.where(lower, 0.0, value)
+
+    def halo_part(phase, side, column, value):
+        cols = slice(column * LANES, (column + 1) * LANES)
+        k = tail(phase, side)
+        return small(sided(phase, side, value), mh[phase, k, cols], ml[phase, k, cols])
+
+    def two(send):
+        return jnp.concatenate([send[0, 1:2, :], send[0, 0:1, :]], axis=1)
+
+    def share(phase, links, weights, start, blocks, indices):
+        for side, index in enumerate(indices):
+            picked(links, start, blocks, index, glink.at[side, phase])
+            picked(weights, start, blocks, index, gweight.at[side, phase])
+
+    picked(xs, n1, b1, sc1[0, 1:2, :], hsend.at[0, 0])
+    picked(xs, n1, b1, sc1[0, 0:1, :], hsend.at[0, 1])
+    share(0, pl1, pw1, 0, b1, (sd1[0, 1:2, :], sd1[0, 0:1, :]))
+    share(1, ul1, uw1, n2, b2, (two(sc2), two(sc2)))
+    share(2, pl2, pw2, 0, b2, (two(sd2), two(sd2)))
     put(ext, padded, 0, xs[:, n1:cells])
     build(pl1, pw1, merged, p1h, p1l, 0, n1, e1 // LANES)
     predict(det1, 0, fine1, (0, n1), p1h, p1l, n1, False)
-    for c in flight:
-        c.wait()
-    land_one(0, n1)
+    picked(det1, 0, b1, sd1[0, 1:2, :], part.at[0])
+    picked(det1, 0, b1, sd1[0, 0:1, :], part.at[1])
+
+    def spread(links, weights, phase, column, blocks, base):
+        build(
+            links, weights, merged, mh.at[phase], ml.at[phase], 0, LANES, blocks, base,
+            column * LANES,
+        )
+
+    for side in range(2):
+        spread(glink.at[side, 0], gweight.at[side, 0], 0, side, h1, b1)
+    build(ul1, uw1, merged, u1h, u1l, n2, n2, e1 // LANES)
+    pl.semaphore_wait(barrier, 2 + n_lev - 1)
+    for side in range(2):
+        copy_to(0, side).start()
+    for side in range(2):
+        for c in meta_to(side):
+            c.start()
+    spread(glink.at[0, 1], gweight.at[0, 1], 1, 0, h1, b1)
+    spread(glink.at[0, 2], gweight.at[0, 2], 2, 0, h2, b2)
+    build(pl2, pw2, merged, p2h, p2l, 0, n2, e2 // LANES)
+
+    def step0(side):
+        copy_to(0, side).wait_recv()
+        hsend[1, side] = part[side] - halo_part(0, side, side, hrecv[0, side])
+        copy_to(1, side).start()
+
+    both_sides(step0)
+    put(ext, padded, n1, hrecv[0, 0])
+    put(ext, padded, n1 + halo1, hrecv[0, 1])
     predict(det1, 0, held(det1), (n1, e1), p1h, p1l, n1, False)
-
-    send_one(1, det1, 0, b1, sd1)
-    flight = swap(1, hsend.at[1, 0], hsend.at[1, 1])
     scatter(det1, 0)
+
     put(ext, padded, 0, det1[...])
-    build(ul1, uw1, merged, u1h, u1l, n2, n2, e1 // LANES)
     predict(sm1, n2, coarse1, (0, n1), u1h, u1l, n2, True)
-    build(pl2, pw2, merged, p2h, p2l, 0, n2, e2 // LANES)
-    for c in flight:
-        c.wait()
-    land_one(1, n1)
+    picked(sm1, n2, b2, two(sc2), part.at[0])
+    picked(det1, 0, b1, sd1[0, 1:2, :], full1.at[0])
+    picked(det1, 0, b1, sd1[0, 0:1, :], full1.at[1])
+    for side in range(2):
+        for c in meta_to(side):
+            c.wait_recv()
+    for side in range(2):
+        spread(rlink.at[side, 0], rweight.at[side, 0], 0, 2 + side, h1, b1)
+
+    def step1(side):
+        copy_to(1, side).wait_recv()
+        value = hrecv[1, side] - halo_part(0, 1 - side, 2 + side, hsend[0, 1 - side])
+        done[side] = value
+        hsend[2, side] = part[0] + halo_part(1, side, 0, value)
+        copy_to(2, side).start()
+
+    both_sides(step1)
+    put(ext, padded, n1, done[0])
+    put(ext, padded, n1 + halo1, done[1])
     predict(sm1, n2, held(sm1), (n1, e1), u1h, u1l, n2, True)
 
-    send_two(2, sm1, n2, b2, sc2)
-    flight = swap(2, hsend.at[2, 0], hsend.at[2, 0])
     build(ul1, uw1, merged, u1h, u1l, 0, n2, e1 // LANES)
     predict(sm1, 0, coarse1, (0, e1), u1h, u1l, n2, True)
-    put(ext, padded, 0, sm1[:, n2:n1])
+    put(ext2, padded, 0, sm1[:, n2:n1])
+    picked(sm1, n2, b2, two(sc2), full2)
     predict(det2, 0, fine2, (0, n2), p2h, p2l, n2, False)
-    for c in flight:
-        c.wait()
-    land_two(2, n2)
+    picked(det2, 0, b2, two(sd2), part.at[1])
+    for side in range(2):
+        spread(rlink.at[side, 1], rweight.at[side, 1], 1, 2 + side, h1, b1)
+
+    def step2(side):
+        copy_to(2, side).wait_recv()
+        value = hrecv[2, side] + halo_part(1, 1 - side, 2 + side, full1[1 - side])
+        done[side] = value
+        hsend[3, side] = part[1] - halo_part(2, side, 0, value)
+        copy_to(3, side).start()
+
+    both_sides(step2)
+    put(ext2, padded, n2, jnp.where(lower, done[0], done[1]))
     predict(det2, 0, held(det2), (n2, e2), p2h, p2l, n2, False)
-
-    send_two(3, det2, 0, b2, sd2)
-    flight = swap(3, hsend.at[3, 0], hsend.at[3, 0])
     scatter(det2, n1)
-    put(ext, padded, 0, det2[...])
+
+    put(ext2, padded, 0, det2[...])
+    for side in range(2):
+        spread(rlink.at[side, 2], rweight.at[side, 2], 2, 2 + side, h2, b2)
     build(ul2, uw2, merged, u2h, u2l, 0, n2, e2 // LANES)
     predict(sm2, 0, coarse2, (0, n2), u2h, u2l, n2, True)
-    for c in flight:
-        c.wait()
-    land_two(3, n2)
+
+    def step3(side):
+        copy_to(3, side).wait_recv()
+        done[side] = hrecv[3, side] - halo_part(2, 1 - side, 2 + side, full2[...])
+
+    both_sides(step3)
+    put(ext2, padded, n2, jnp.where(lower, done[0], done[1]))
     predict(sm2, 0, held(sm2), (n2, e2), u2h, u2l, n2, True)
     scatter(sm2, n1 + n2)
 
@@ -292,6 +387,11 @@
                 device_id_type=MESH,
             ).wait_recv()
 
+    for side in range(2):
+        for phase in range(4):
+            copy_to(phase, side).wait_send()
+        for c in meta_to(side):
+            c.wait_send()
     for d, copy in outgoing:
 
         @pl.when(me != d)
@@ -348,6 +448,19 @@
             pltpu.VMEM((padded, n2), f32),
             pltpu.VMEM((4, 2, padded, LANES), f32),
             pltpu.VMEM((4, 2, padded, LANES), f32),
+            pltpu.VMEM((2 * padded, e2), bf16),
+            pltpu.VMEM((2, 3, slots, LANES), jnp.int32),
+            pltpu.VMEM((2, 3, slots, LANES), f32),
+            pltpu.VMEM((2, 3, slots, LANES), jnp.int32),
+            pltpu.VMEM((2, 3, slots, LANES), f32),
+            pltpu.VMEM((3, 2 * LANES, 4 * LANES), bf16),
+            pltpu.VMEM((3, 2 * LANES, 4 * LANES), bf16),
+            pltpu.VMEM((2, padded, LANES), f32),
+            pltpu.VMEM((2, padded, LANES), f32),
+            pltpu.VMEM((padded, LANES), f32),
+            pltpu.VMEM((2, padded, LANES), f32),
+            pltpu.SemaphoreType.DMA((2, 2)),
+            pltpu.SemaphoreType.DMA((2, 2)),
             pltpu.SemaphoreType.DMA((4, 2)),
             pltpu.SemaphoreType.DMA((4, 2)),
             pltpu.SemaphoreType.DMA((n_lev,)),

time: 31.6 us -> 32.8 us (1.038)
  Pallas kernels: 31.5 us -> 32.6 us
    pallas_call x1, Pallas kernels: 29 us -> 30.2 us  [on_device(): pl.pallas_call(functools.partial(body, n_patch, n_lev, levels), out_shape...]
where the time goes in v3:
time: 32.8 us; the launch traced here: 32.6 us
  Pallas kernels  32.6 us (99%)
    pallas_call x1, Pallas kernels, on_device(): pl.pallas_call(functools.partial(body, n_patch, n_lev, levels), out_shape...  30.2 us
    pallas_call x1, Pallas kernels, on_device(): pl.pallas_call(transform, out_shape=jax.ShapeDtypeStruct((tracers, levels...  2.46 us

profile of v3, /device:TPU:0, one launch (start us, length us, event | category | flops | bytes accessed | tf_op | source)
XLA Modules:
  0.0 32.6 jit_solution(2781510288691160174)
XLA Ops:
  0.0 30.2 %shard_map.145.gathered = f32[4,64,512]{2,1,0:T(8,128)} custom-call(f32[3,20,2048]{2,1,0:T(8,128)} %bitcast.2, s32[1,2,128]{2,1,0:T(2,128)} %sc1.1, s32[1,2,128]{2,1,0:T(2,128)} %sd1.1, s32[1,2,64]{2,1,0:T(2,128)} %sc2.1, s32[1,2,64]{2,1,0:T(2,128)} %sd2.1, s32[8,1024]{1,0:T(8,128)} %pl1.1, f32[8,1024]{1,0:T(8,128)} %pw1.1, s32[8,1024]{1,0:T(8,128)} %ul1.1, ...), custom_call_target="tpu_custom_call" | custom-call | tf_op jit(solution)/shard_map/pallas_call | solution.py:428
  30.2 2.5 %shard_map.146 = f32[3,80,512]{2,1,0:T(8,128)} custom-call(f32[4,64,512]{2,1,0:T(8,128)} %shard_map.145.gathered, bf16[240,256]{1,0:T(8,128)(2,1)} %constant.4.clone.t_high, bf16[240,256]{1,0:T(8,128)(2,1)} %constant.5.clone.t_low), custom_call_target="tpu_custom_call" | custom-call | tf_op jit(solution)/shard_map/pallas_call | solution.py:471

commit v4 on v3

--- a/solution.py
+++ b/solution.py
@@ -276,9 +276,15 @@
 
     picked(xs, n1, b1, sc1[0, 1:2, :], hsend.at[0, 0])
     picked(xs, n1, b1, sc1[0, 0:1, :], hsend.at[0, 1])
+    pl.semaphore_wait(barrier, 2 + n_lev - 1)
+    for side in range(2):
+        copy_to(0, side).start()
     share(0, pl1, pw1, 0, b1, (sd1[0, 1:2, :], sd1[0, 0:1, :]))
     share(1, ul1, uw1, n2, b2, (two(sc2), two(sc2)))
     share(2, pl2, pw2, 0, b2, (two(sd2), two(sd2)))
+    for side in range(2):
+        for c in meta_to(side):
+            c.start()
     put(ext, padded, 0, xs[:, n1:cells])
     build(pl1, pw1, merged, p1h, p1l, 0, n1, e1 // LANES)
     predict(det1, 0, fine1, (0, n1), p1h, p1l, n1, False)
@@ -293,16 +299,6 @@
 
     for side in range(2):
         spread(glink.at[side, 0], gweight.at[side, 0], 0, side, h1, b1)
-    build(ul1, uw1, merged, u1h, u1l, n2, n2, e1 // LANES)
-    pl.semaphore_wait(barrier, 2 + n_lev - 1)
-    for side in range(2):
-        copy_to(0, side).start()
-    for side in range(2):
-        for c in meta_to(side):
-            c.start()
-    spread(glink.at[0, 1], gweight.at[0, 1], 1, 0, h1, b1)
-    spread(glink.at[0, 2], gweight.at[0, 2], 2, 0, h2, b2)
-    build(pl2, pw2, merged, p2h, p2l, 0, n2, e2 // LANES)
 
     def step0(side):
         copy_to(0, side).wait_recv()
@@ -315,6 +311,8 @@
     predict(det1, 0, held(det1), (n1, e1), p1h, p1l, n1, False)
     scatter(det1, 0)
 
+    spread(glink.at[0, 1], gweight.at[0, 1], 1, 0, h1, b1)
+    build(ul1, uw1, merged, u1h, u1l, n2, n2, e1 // LANES)
     put(ext, padded, 0, det1[...])
     predict(sm1, n2, coarse1, (0, n1), u1h, u1l, n2, True)
     picked(sm1, n2, b2, two(sc2), part.at[0])
@@ -338,6 +336,8 @@
     put(ext, padded, n1 + halo1, done[1])
     predict(sm1, n2, held(sm1), (n1, e1), u1h, u1l, n2, True)
 
+    spread(glink.at[0, 2], gweight.at[0, 2], 2, 0, h2, b2)
+    build(pl2, pw2, merged, p2h, p2l, 0, n2, e2 // LANES)
     build(ul1, uw1, merged, u1h, u1l, 0, n2, e1 // LANES)
     predict(sm1, 0, coarse1, (0, e1), u1h, u1l, n2, True)
     put(ext2, padded, 0, sm1[:, n2:n1])

time: 32.8 us -> 31.5 us (0.960)
  Pallas kernels: 32.6 us -> 31.4 us
    pallas_call x1, Pallas kernels: 30.2 us -> 28.9 us  [on_device(): pl.pallas_call(functools.partial(body, n_patch, n_lev, levels), out_shape...]
where the time goes in v4:
time: 31.5 us; the launch traced here: 31.4 us
  Pallas kernels  31.4 us (100%)
    pallas_call x1, Pallas kernels, on_device(): pl.pallas_call(functools.partial(body, n_patch, n_lev, levels), out_shape...  28.9 us
    pallas_call x1, Pallas kernels, on_device(): pl.pallas_call(transform, out_shape=jax.ShapeDtypeStruct((tracers, levels...  2.46 us

profile of v4, /device:TPU:0, one launch (start us, length us, event | category | flops | bytes accessed | tf_op | source)
XLA Modules:
  0.0 31.4 jit_solution(8944053375932331477)
XLA Ops:
  0.0 28.9 %shard_map.145.gathered = f32[4,64,512]{2,1,0:T(8,128)} custom-call(f32[3,20,2048]{2,1,0:T(8,128)} %bitcast.2, s32[1,2,128]{2,1,0:T(2,128)} %sc1.1, s32[1,2,128]{2,1,0:T(2,128)} %sd1.1, s32[1,2,64]{2,1,0:T(2,128)} %sc2.1, s32[1,2,64]{2,1,0:T(2,128)} %sd2.1, s32[8,1024]{1,0:T(8,128)} %pl1.1, f32[8,1024]{1,0:T(8,128)} %pw1.1, s32[8,1024]{1,0:T(8,128)} %ul1.1, ...), custom_call_target="tpu_custom_call" | custom-call | tf_op jit(solution)/shard_map/pallas_call | solution.py:428
  28.9 2.5 %shard_map.146 = f32[3,80,512]{2,1,0:T(8,128)} custom-call(f32[4,64,512]{2,1,0:T(8,128)} %shard_map.145.gathered, bf16[240,256]{1,0:T(8,128)(2,1)} %constant.4.clone.t_high, bf16[240,256]{1,0:T(8,128)(2,1)} %constant.5.clone.t_low), custom_call_target="tpu_custom_call" | custom-call | tf_op jit(solution)/shard_map/pallas_call | solution.py:471

commit v5 on v4

--- a/solution.py
+++ b/solution.py
@@ -323,6 +323,10 @@
             c.wait_recv()
     for side in range(2):
         spread(rlink.at[side, 0], rweight.at[side, 0], 0, 2 + side, h1, b1)
+    spread(glink.at[0, 2], gweight.at[0, 2], 2, 0, h2, b2)
+    build(pl2, pw2, merged, p2h, p2l, 0, n2, e2 // LANES)
+    for side in range(2):
+        spread(rlink.at[side, 1], rweight.at[side, 1], 1, 2 + side, h1, b1)
 
     def step1(side):
         copy_to(1, side).wait_recv()
@@ -336,16 +340,12 @@
     put(ext, padded, n1 + halo1, done[1])
     predict(sm1, n2, held(sm1), (n1, e1), u1h, u1l, n2, True)
 
-    spread(glink.at[0, 2], gweight.at[0, 2], 2, 0, h2, b2)
-    build(pl2, pw2, merged, p2h, p2l, 0, n2, e2 // LANES)
     build(ul1, uw1, merged, u1h, u1l, 0, n2, e1 // LANES)
     predict(sm1, 0, coarse1, (0, e1), u1h, u1l, n2, True)
     put(ext2, padded, 0, sm1[:, n2:n1])
     picked(sm1, n2, b2, two(sc2), full2)
     predict(det2, 0, fine2, (0, n2), p2h, p2l, n2, False)
     picked(det2, 0, b2, two(sd2), part.at[1])
-    for side in range(2):
-        spread(rlink.at[side, 1], rweight.at[side, 1], 1, 2 + side, h1, b1)
 
     def step2(side):
         copy_to(2, side).wait_recv()

time: 31.5 us -> 30.3 us (0.962)
  Pallas kernels: 31.4 us -> 30.1 us
    pallas_call x1, Pallas kernels: 28.9 us -> 27.7 us  [on_device(): pl.pallas_call(functools.partial(body, n_patch, n_lev, levels), out_shape...]
where the time goes in v5:
time: 30.3 us; the launch traced here: 30.1 us
  Pallas kernels  30.1 us (99%)
    pallas_call x1, Pallas kernels, on_device(): pl.pallas_call(functools.partial(body, n_patch, n_lev, levels), out_shape...  27.7 us
    pallas_call x1, Pallas kernels, on_device(): pl.pallas_call(transform, out_shape=jax.ShapeDtypeStruct((tracers, levels...  2.46 us

profile of v5, /device:TPU:0, one launch (start us, length us, event | category | flops | bytes accessed | tf_op | source)
XLA Modules:
  0.0 30.1 jit_solution(7099970555215190196)
XLA Ops:
  0.0 27.7 %shard_map.145.gathered = f32[4,64,512]{2,1,0:T(8,128)} custom-call(f32[3,20,2048]{2,1,0:T(8,128)} %bitcast.2, s32[1,2,128]{2,1,0:T(2,128)} %sc1.1, s32[1,2,128]{2,1,0:T(2,128)} %sd1.1, s32[1,2,64]{2,1,0:T(2,128)} %sc2.1, s32[1,2,64]{2,1,0:T(2,128)} %sd2.1, s32[8,1024]{1,0:T(8,128)} %pl1.1, f32[8,1024]{1,0:T(8,128)} %pw1.1, s32[8,1024]{1,0:T(8,128)} %ul1.1, ...), custom_call_target="tpu_custom_call" | custom-call | tf_op jit(solution)/shard_map/pallas_call | solution.py:428
  27.7 2.5 %shard_map.146 = f32[3,80,512]{2,1,0:T(8,128)} custom-call(f32[4,64,512]{2,1,0:T(8,128)} %shard_map.145.gathered, bf16[240,256]{1,0:T(8,128)(2,1)} %constant.4.clone.t_high, bf16[240,256]{1,0:T(8,128)(2,1)} %constant.5.clone.t_low), custom_call_target="tpu_custom_call" | custom-call | tf_op jit(solution)/shard_map/pallas_call | solution.py:471
